TPU v7x, 256 devices: a whole 4x4x8 slice. The times are simulated.
256 devices in a mesh: row: 16 (over x, z_hi), col: 16 (over y, z_lo, core).
Axes of the slice: x: 4, y: 4, z: 8 (z_hi: 4, z_lo: 2; z = z_hi * 2 + z_lo), core: 2. Of those that a mesh axis runs over, the one named last changes fastest.
Arguments:
- tile_count: int32 [16, 16], P('row', 'col'), may hold values from 1 to 40, as said below
- tile_rows: int32 [16, 16, 40], P('row', 'col'), may hold values from 0 to 31, as said below
- tile_cols: int32 [16, 16, 40], P('row', 'col'), may hold values from 0 to 31, as said below
- tiles: float32 [16, 16, 40, 256, 256], P('row', 'col')
- block: float32 [64, 131072], P(None, ('row', 'col')), may hold values from -6 to 6
Outputs:
- image_x: float32 [64, 131072], P(None, ('row', 'col'))
- image_w: float32 [64, 131072], P(None, ('row', 'col'))
- grams: float32 [4, 64, 64], replicated
Inputs may be any that keep to these rules, and one draw needn't show every extreme that they name: `tile_count`: live slots of each grid block; the largest count over the grid is exactly 40. `tile_rows`: live slots of one grid block hold distinct positions whose global tile row is at least the global tile column; slots at or past the count hold 0. `tile_cols`: paired with tile_rows as above; slots at or past the count hold 0.
All inputs are finite; a program needn't handle non-finite values.
Results may differ from a plain program's by a relative error of at most 0.0001.
Values sent between devices are 32-bit elements; how exact they have to be, the bound alone decides.
A program may use at most 64 MiB of HBM per device.

v0:
```python
import jax
import jax.numpy as jnp
from jax import lax
from jax.sharding import PartitionSpec as P

highest = lax.Precision.HIGHEST


def passed_along(array, axis, by):
    size = lax.axis_size(axis)
    return lax.ppermute(array, axis, [(i, (i + by) % size) for i in range(size)])


def inner_prod(left, right):
    return lax.dot_general(
        left, right, (((1,), (1,)), ((), ())), precision=highest, preferred_element_type=jnp.float32
    )


def on_device(tile_count, tile_rows, tile_cols, tiles, block):
    vec_count, seg_rows = block.shape
    tile_size = tiles.shape[-1]
    seg_tiles = seg_rows // tile_size
    grid_rows = lax.axis_size("row")
    grid_cols = lax.axis_size("col")
    total_rows = seg_rows * grid_rows * grid_cols
    live_count = tile_count[0, 0]
    row_ids = tile_rows[0, 0]
    col_ids = tile_cols[0, 0]
    tile_data = tiles[0, 0]
    row_slots = grid_cols * seg_tiles
    col_slots = grid_rows * seg_tiles

    def expand(vectors):
        near_vec = lax.all_gather(vectors, "col", axis=1, tiled=True)
        far_vec = lax.all_gather(vectors, "row", axis=1, tiled=True)
        near_tiles = near_vec.reshape(vec_count, row_slots, tile_size)
        far_tiles = far_vec.reshape(vec_count, col_slots, tile_size)
        groups = (live_count + 7) // 8

        def accumulate(counter, carry):
            sums_rows, sums_cols = carry
            offset = counter * 8
            block_tiles = lax.dynamic_slice_in_dim(tile_data, offset, 8, 0)
            slot_rows = lax.dynamic_slice_in_dim(row_ids, offset, 8, 0)
            slot_cols = lax.dynamic_slice_in_dim(col_ids, offset, 8, 0)
            live_mask = (offset + jnp.arange(8, dtype=jnp.int32) < live_count).astype(jnp.float32)
            rows_in = jnp.take(near_tiles, slot_rows, axis=1)
            cols_in = jnp.take(far_tiles, slot_cols, axis=1)
            lower_part = (
                jnp.einsum("sij,ksj->ksi", block_tiles, cols_in, precision=highest)
                * live_mask[None, :, None]
            )
            upper_part = (
                jnp.einsum("sij,ksi->ksj", block_tiles, rows_in, precision=highest)
                * live_mask[None, :, None]
            )
            row_pick = (
                slot_rows[:, None] == jnp.arange(row_slots, dtype=jnp.int32)[None, :]
            ).astype(jnp.float32)
            col_pick = (
                slot_cols[:, None] == jnp.arange(col_slots, dtype=jnp.int32)[None, :]
            ).astype(jnp.float32)
            sums_rows = sums_rows + jnp.einsum(
                "ksi,sp->kpi", lower_part, row_pick, precision=highest
            )
            sums_cols = sums_cols + jnp.einsum(
                "ksi,sp->kpi", upper_part, col_pick, precision=highest
            )
            return (sums_rows, sums_cols)

        empty_rows = jnp.zeros((vec_count, row_slots, tile_size), jnp.float32)
        empty_cols = jnp.zeros((vec_count, col_slots, tile_size), jnp.float32)
        part_rows, part_cols = lax.fori_loop(0, groups, accumulate, (empty_rows, empty_cols))
        return (
            near_vec,
            far_vec,
            part_rows.reshape(vec_count, row_slots * tile_size),
            part_cols.reshape(vec_count, col_slots * tile_size),
        )

    def combine_sums(part_rows, part_cols):
        pieces_rows = part_rows.reshape(vec_count, grid_cols, seg_rows)
        pieces_cols = part_cols.reshape(vec_count, grid_rows, seg_rows)
        my_col = lax.axis_index("col")
        my_row = lax.axis_index("row")

        def select_piece(pieces, position):
            return lax.dynamic_index_in_dim(pieces, position, 1, keepdims=False)

        def pass_along_rows(counter, running):
            moved = passed_along(running, "col", 1)
            return moved + select_piece(
                pieces_rows, (my_col + 2 * grid_cols - 1 - counter) % grid_cols
            )

        def pass_along_cols(counter, running):
            moved = passed_along(running, "row", 1)
            return moved + select_piece(
                pieces_cols, (my_row + 2 * grid_rows - 1 - counter) % grid_rows
            )

        first_rows = select_piece(pieces_rows, (my_col + grid_cols - 1) % grid_cols)
        first_cols = select_piece(pieces_cols, (my_row + grid_rows - 1) % grid_rows)
        own_rows = lax.fori_loop(1, grid_cols, pass_along_rows, first_rows)
        own_cols = lax.fori_loop(1, grid_rows, pass_along_cols, first_cols)
        return own_rows + own_cols

    near_x, far_x, rows_x, cols_x = expand(block)
    image_x = combine_sums(rows_x, cols_x)
    first_term = inner_prod(block, image_x)
    rayleigh = lax.psum(first_term, ("row", "col")) / total_rows
    resid = image_x - jnp.dot(
        rayleigh, block, precision=highest, preferred_element_type=jnp.float32
    )
    near_w, far_w, rows_w, cols_w = expand(resid)
    image_w = combine_sums(rows_w, cols_w)
    cross_term = inner_prod(block, image_w)
    resid_term = inner_prod(resid, image_w)
    square_term = inner_prod(resid, resid)
    others = lax.psum(jnp.stack([cross_term, resid_term, square_term]), ("row", "col")) / total_rows
    grams = jnp.concatenate([rayleigh[None], others], axis=0)
    return (image_x, image_w, grams)


def solution(mesh):
    return jax.shard_map(
        on_device,
        mesh=mesh,
        in_specs=(
            P("row", "col"),
            P("row", "col", None),
            P("row", "col", None),
            P("row", "col", None, None, None),
            P(None, ("row", "col")),
        ),
        out_specs=(P(None, ("row", "col")), P(None, ("row", "col")), P()),
        check_vma=False,
    )
```

profile of v0, /device:TPU:1, one launch (start us, length us, event | category | flops | bytes accessed | tf_op | source)
XLA Modules:
  0.0 1077.0 jit_solution(5392531176664811493)
XLA Ops:
  9.4 40.8 %all-gather.7.cloned.1.call-done = f32[64,8192]{1,0:T(8,128)} async-done(((f32[64,512]{1,0:T(8,128)}), f32[64,8192]{1,0:T(8,128)}) %all-gather.7.cloned.1.call-update) | async-done | bytes 2097168 | tf_op jit(solution)/shard_map/all_gather | solution.py:35
  53.4 56.9 %all-gather.5.cloned.1.call-done = f32[64,8192]{1,0:T(8,128)} async-done(((f32[64,512]{1,0:T(8,128)}), f32[64,8192]{1,0:T(8,128)}) %all-gather.5.cloned.1.call-update) | async-done | bytes 2097168 | tf_op jit(solution)/shard_map/all_gather | solution.py:36
  115.4 17.8 %while.84 = (s32[]{:T(128)}, f32[64,32,256]{2,1,0:T(8,128)S(1)}, f32[64,32,256]{2,1,0:T(8,128)}, s32[]{:T(128)}, s32[40]{0:T(128)S(1)}, /*index=5*/s32[40]{0:T(1...) while((s32[]{:T(128)}, f32[64,32,256]{2,1,0:T(8,128)S(1)}, ...), condition=%wide.region_1.3_spmd, body=%wide.region_0.2_spmd.sunk | while | flops 907545280 | bytes 17834760 | solution.py:74
  140.4 217.7 %while.86 = (s32[]{:T(128)}, f32[64,512]{1,0:T(8,128)S(1)}, s32[]{:T(128)}, f32[64,16,512]{2,1,0:T(8,128)}, s32[]{:T(128)}, /*index=5*/s32[]{:T(128)}, s32[]{:T(128)}, s32[]{:T(128)}) while((s32[]{:T(128)}, f32[64,512]{1,0:T(8,128)S(1)}, s32[]{:T(128)}, f32[64,16,512]{2,1,0:T(8,128)}, s32[]{:T(128)}, /*index=5*/s32[]{:T(128)}, s32[]{:T(128)}, ...), condition=%wide.region_5.7_spmd, body=%wide.region_4.6_spmd.sunk | while | flops 32785 | bytes 1179932 | solution.py:106
  143.3 75.8 %collective-permute-done.1 = f32[64,512]{1,0:T(8,128)S(1)} collective-permute-done((f32[64,512]{1,0:T(8,128)S(1)}, f32[64,512]{1,0:T(8,128)S(1)}, u32[]{:S(2)}, u32[]{:S(2)}) %collective-permute-start.1) | collective-permute-done | bytes 131104 | tf_op jit(solution)/shard_map/while/body/eval_jaxpr/ppermute | solution.py:11
  220.6 6.7 collective-permute-done.1
  228.7 6.7 collective-permute-done.1
  236.9 7.4 collective-permute-done.1
  245.8 9.6 collective-permute-done.1
  256.9 7.4 collective-permute-done.1
  265.8 9.0 collective-permute-done.1
  276.3 9.1 collective-permute-done.1
  286.9 10.8 %collective-permute-done.1 = f32[64,512]{1,0:T(8,128)S(1)} collective-permute-done((f32[64,512]{1,0:T(8,128)S(1)}, f32[64,512]{1,0:T(8,128)S(1)}, u32[]{:S(2)}, u32[]{:S(2)}) %collective-permute-start.1) | collective-permute-done | bytes 131104 | tf_op jit(solution)/shard_map/while/body/eval_jaxpr/ppermute | solution.py:11
  299.2 9.9 collective-permute-done.1
  310.6 8.7 collective-permute-done.1
  320.8 10.4 collective-permute-done.1
  332.7 8.9 collective-permute-done.1
  343.1 6.8 collective-permute-done.1
  351.4 6.7 collective-permute-done.1
  358.1 108.0 %while.85 = (s32[]{:T(128)}, f32[64,512]{1,0:T(8,128)S(1)}, s32[]{:T(128)}, f32[64,16,512]{2,1,0:T(8,128)}, s32[]{:T(128)}, /*index=5*/s32[]{:T(128)}, s32[]{:T(128)}, s32[]{:T(128)}) while((s32[]{:T(128)}, f32[64,512]{1,0:T(8,128)S(1)}, s32[]{:T(128)}, f32[64,16,512]{2,1,0:T(8,128)}, s32[]{:T(128)}, /*index=5*/s32[]{:T(128)}, s32[]{:T(128)}, ...), condition=%wide.region_3.5_spmd, body=%wide.region_2.4_spmd.sunk | while | flops 32785 | bytes 1179932 | solution.py:105
  358.1 9.1 collective-permute-start
  374.9 5.1 collective-permute-done
  381.6 5.1 collective-permute-done
  388.2 5.1 collective-permute-done
  394.8 5.1 collective-permute-done
  466.4 76.2 %psum.14 = f32[64,64]{0,1:T(8,128)S(1)} all-reduce(f32[64,64]{0,1:T(8,128)S(1)} %convolution_bitcast_fusion.3), channel_id=1, replica_groups=mesh['row'=16,'col'=16] {'row','col'}, use_global_device_ids=true, to_apply=%region_6.8 | all-reduce | flops 4096 | bytes 32768 | tf_op jit(solution)/shard_map/psum | solution.py:112
  545.5 30.2 %all-gather.11.cloned.1.call-done = f32[64,8192]{1,0:T(8,128)} async-done(((f32[64,512]{1,0:T(8,128)}), f32[64,8192]{1,0:T(8,128)}) %all-gather.11.cloned.1.call-update) | async-done | bytes 2097168 | tf_op jit(solution)/shard_map/all_gather | solution.py:35
  578.9 57.3 %all-gather.9.cloned.1.call-done = f32[64,8192]{1,0:T(8,128)} async-done(((f32[64,512]{1,0:T(8,128)}), f32[64,8192]{1,0:T(8,128)}) %all-gather.9.cloned.1.call-update) | async-done | bytes 2097168 | tf_op jit(solution)/shard_map/all_gather | solution.py:36
  641.3 17.8 %while.87 = (s32[]{:T(128)}, f32[64,32,256]{2,1,0:T(8,128)S(1)}, f32[64,32,256]{2,1,0:T(8,128)}, s32[]{:T(128)}, s32[40]{0:T(128)S(1)}, /*index=5*/s32[40]{0:T(1...) while((s32[]{:T(128)}, f32[64,32,256]{2,1,0:T(8,128)S(1)}, ...), condition=%wide.region_8.10_spmd, body=%wide.region_7.9_spmd.sunk | while | flops 907545280 | bytes 17834760 | solution.py:74
  666.3 222.1 %while.89 = (s32[]{:T(128)}, f32[64,512]{1,0:T(8,128)S(1)}, s32[]{:T(128)}, f32[64,16,512]{2,1,0:T(8,128)}, s32[]{:T(128)}, /*index=5*/s32[]{:T(128)}, s32[]{:T(128)}, s32[]{:T(128)}) while((s32[]{:T(128)}, f32[64,512]{1,0:T(8,128)S(1)}, s32[]{:T(128)}, f32[64,16,512]{2,1,0:T(8,128)}, s32[]{:T(128)}, /*index=5*/s32[]{:T(128)}, s32[]{:T(128)}, ...), condition=%wide.region_12.14_spmd, body=%wide.region_11.13_spmd.sunk | while | flops 32785 | bytes 1179932 | solution.py:106
  669.2 75.8 %collective-permute-done.3 = f32[64,512]{1,0:T(8,128)S(1)} collective-permute-done((f32[64,512]{1,0:T(8,128)S(1)}, f32[64,512]{1,0:T(8,128)S(1)}, u32[]{:S(2)}, u32[]{:S(2)}) %collective-permute-start.3) | collective-permute-done | bytes 131104 | tf_op jit(solution)/shard_map/while/body/eval_jaxpr/ppermute | solution.py:11
  746.5 6.7 collective-permute-done.3
  754.6 6.7 collective-permute-done.3
  762.8 7.5 collective-permute-done.3
  771.8 9.6 collective-permute-done.3
  782.9 7.4 collective-permute-done.3
  791.8 9.2 collective-permute-done.3
  802.5 8.7 collective-permute-done.3
  812.7 10.7 collective-permute-done.3
  824.8 10.1 collective-permute-done.3
  836.4 8.7 collective-permute-done.3
  846.6 10.4 collective-permute-done.3
  858.6 8.6 collective-permute-done.3
  868.7 9.3 collective-permute-done.3
  879.4 8.9 collective-permute-done.3
  888.4 104.1 %while.88 = (s32[]{:T(128)}, f32[64,512]{1,0:T(8,128)S(1)}, s32[]{:T(128)}, f32[64,16,512]{2,1,0:T(8,128)}, s32[]{:T(128)}, /*index=5*/s32[]{:T(128)}, s32[]{:T(128)}, s32[]{:T(128)}) while((s32[]{:T(128)}, f32[64,512]{1,0:T(8,128)S(1)}, s32[]{:T(128)}, f32[64,16,512]{2,1,0:T(8,128)}, s32[]{:T(128)}, /*index=5*/s32[]{:T(128)}, s32[]{:T(128)}, ...), condition=%wide.region_10.12_spmd, body=%wide.region_9.11_spmd.sunk | while | flops 32785 | bytes 1179932 | solution.py:105
  894.4 5.5 collective-permute-done.2
  993.1 76.6 %psum.15 = f32[3,64,64]{1,2,0:T(8,128)S(1)} all-reduce(f32[3,64,64]{1,2,0:T(8,128)S(1)} %pad_maximum_fusion.1), channel_id=1, replica_groups=mesh['row'=16,'col'=16] {'row','col'}, use_global_device_ids=true, to_apply=%region_13.15 | all-reduce | flops 12288 | bytes 98304 | tf_op jit(solution)/shard_map/psum | solution.py:121
  (280 shorter events, 294.1 us)
Async XLA Ops:
  7.2 43.1 %all-gather.7.cloned.1.call-start = ((), (), s32[]{:S(2)}) async-start(), calls=%async_computation.1 | async-start | bytes 2228224 | tf_op jit(solution)/shard_map/all_gather | solution.py:35
  7.9 102.4 %all-gather.5.cloned.1.call-start = ((), (), s32[]{:S(2)}) async-start(), calls=%async_computation | async-start | bytes 2228224 | tf_op jit(solution)/shard_map/all_gather | solution.py:36
  8.6 567.1 %all-gather.11.cloned.1.call-start = ((), (), s32[]{:S(2)}) async-start(), calls=%async_computation.3 | async-start | bytes 2228224 | tf_op jit(solution)/shard_map/all_gather | solution.py:35
  140.4 78.7 %collective-permute-start.1 = (f32[64,512]{1,0:T(8,128)S(1)}, f32[64,512]{1,0:T(8,128)S(1)}, u32[]{:S(2)}, u32[]{:S(2)}) collective-permute-start(f32[64,512]{1,0:T(8,128)S(1)} %get-tuple-element.1050), channel_id=1, source_target_pairs={{0,16},{16,32},{32,48},{48,64},{64,80},{80,96},{96,112},{112,128},... | collective-permute-start | bytes 393224 | tf_op jit(solution)/shard_map/while/body/eval_jaxpr/ppermute | solution.py:11
  219.1 8.1 collective-permute-start.1
  227.3 8.1 collective-permute-start.1
  235.4 8.9 collective-permute-start.1
  244.4 11.1 %collective-permute-start.1 = (f32[64,512]{1,0:T(8,128)S(1)}, f32[64,512]{1,0:T(8,128)S(1)}, u32[]{:S(2)}, u32[]{:S(2)}) collective-permute-start(f32[64,512]{1,0:T(8,128)S(1)} %get-tuple-element.1050), channel_id=1, source_target_pairs={{0,16},{16,32},{32,48},{48,64},{64,80},{80,96},{96,112},{112,128},... | collective-permute-start | bytes 393224 | tf_op jit(solution)/shard_map/while/body/eval_jaxpr/ppermute | solution.py:11
  255.5 8.9 collective-permute-start.1
  264.4 10.5 collective-permute-start.1
  274.9 10.5 collective-permute-start.1
  285.4 12.3 %collective-permute-start.1 = (f32[64,512]{1,0:T(8,128)S(1)}, f32[64,512]{1,0:T(8,128)S(1)}, u32[]{:S(2)}, u32[]{:S(2)}) collective-permute-start(f32[64,512]{1,0:T(8,128)S(1)} %get-tuple-element.1050), channel_id=1, source_target_pairs={{0,16},{16,32},{32,48},{48,64},{64,80},{80,96},{96,112},{112,128},... | collective-permute-start | bytes 393224 | tf_op jit(solution)/shard_map/while/body/eval_jaxpr/ppermute | solution.py:11
  297.7 11.4 %collective-permute-start.1 = (f32[64,512]{1,0:T(8,128)S(1)}, f32[64,512]{1,0:T(8,128)S(1)}, u32[]{:S(2)}, u32[]{:S(2)}) collective-permute-start(f32[64,512]{1,0:T(8,128)S(1)} %get-tuple-element.1050), channel_id=1, source_target_pairs={{0,16},{16,32},{32,48},{48,64},{64,80},{80,96},{96,112},{112,128},... | collective-permute-start | bytes 393224 | tf_op jit(solution)/shard_map/while/body/eval_jaxpr/ppermute | solution.py:11
  309.2 10.1 collective-permute-start.1
  319.3 11.9 %collective-permute-start.1 = (f32[64,512]{1,0:T(8,128)S(1)}, f32[64,512]{1,0:T(8,128)S(1)}, u32[]{:S(2)}, u32[]{:S(2)}) collective-permute-start(f32[64,512]{1,0:T(8,128)S(1)} %get-tuple-element.1050), channel_id=1, source_target_pairs={{0,16},{16,32},{32,48},{48,64},{64,80},{80,96},{96,112},{112,128},... | collective-permute-start | bytes 393224 | tf_op jit(solution)/shard_map/while/body/eval_jaxpr/ppermute | solution.py:11
  331.3 10.3 collective-permute-start.1
  341.6 8.2 collective-permute-start.1
  349.9 8.1 collective-permute-start.1
  358.1 15.4 %collective-permute-start = (f32[64,512]{1,0:T(8,128)S(1)}, f32[64,512]{1,0:T(8,128)S(1)}, u32[]{:S(2)}, u32[]{:S(2)}) collective-permute-start(f32[64,512]{1,0:T(8,128)S(1)} %get-tuple-element.1026), channel_id=1, source_target_pairs={{0,1},{1,2},{2,3},{3,4},{4,5},{5,6},{6,7},{7,8},{8,9},{9,10},{10,1... | collective-permute-start | bytes 393224 | tf_op jit(solution)/shard_map/while/body/eval_jaxpr/ppermute | solution.py:11
  373.5 6.6 collective-permute-start
  380.1 6.6 collective-permute-start
  386.7 6.6 collective-permute-start
  393.3 6.6 collective-permute-start
  399.9 6.6 collective-permute-start
  406.6 6.6 collective-permute-start
  413.2 6.6 collective-permute-start
  419.8 6.6 collective-permute-start
  426.4 6.6 collective-permute-start
  433.0 6.6 collective-permute-start
  439.6 6.6 collective-permute-start
  446.2 6.6 collective-permute-start
  543.6 92.6 %all-gather.9.cloned.1.call-start = ((), (), s32[]{:S(2)}) async-start(), calls=%async_computation.2 | async-start | bytes 2228224 | tf_op jit(solution)/shard_map/all_gather | solution.py:36
  666.3 78.7 %collective-permute-start.3 = (f32[64,512]{1,0:T(8,128)S(1)}, f32[64,512]{1,0:T(8,128)S(1)}, u32[]{:S(2)}, u32[]{:S(2)}) collective-permute-start(f32[64,512]{1,0:T(8,128)S(1)} %get-tuple-element.1140), channel_id=1, source_target_pairs={{0,16},{16,32},{32,48},{48,64},{64,80},{80,96},{96,112},{112,128},... | collective-permute-start | bytes 393224 | tf_op jit(solution)/shard_map/while/body/eval_jaxpr/ppermute | solution.py:11
  745.0 8.1 collective-permute-start.3
  753.2 8.1 collective-permute-start.3
  761.3 8.9 collective-permute-start.3
  770.3 11.1 %collective-permute-start.3 = (f32[64,512]{1,0:T(8,128)S(1)}, f32[64,512]{1,0:T(8,128)S(1)}, u32[]{:S(2)}, u32[]{:S(2)}) collective-permute-start(f32[64,512]{1,0:T(8,128)S(1)} %get-tuple-element.1140), channel_id=1, source_target_pairs={{0,16},{16,32},{32,48},{48,64},{64,80},{80,96},{96,112},{112,128},... | collective-permute-start | bytes 393224 | tf_op jit(solution)/shard_map/while/body/eval_jaxpr/ppermute | solution.py:11
  781.4 8.9 collective-permute-start.3
  790.3 10.7 collective-permute-start.3
  801.0 10.1 collective-permute-start.3
  811.2 12.1 %collective-permute-start.3 = (f32[64,512]{1,0:T(8,128)S(1)}, f32[64,512]{1,0:T(8,128)S(1)}, u32[]{:S(2)}, u32[]{:S(2)}) collective-permute-start(f32[64,512]{1,0:T(8,128)S(1)} %get-tuple-element.1140), channel_id=1, source_target_pairs={{0,16},{16,32},{32,48},{48,64},{64,80},{80,96},{96,112},{112,128},... | collective-permute-start | bytes 393224 | tf_op jit(solution)/shard_map/while/body/eval_jaxpr/ppermute | solution.py:11
  823.4 11.5 %collective-permute-start.3 = (f32[64,512]{1,0:T(8,128)S(1)}, f32[64,512]{1,0:T(8,128)S(1)}, u32[]{:S(2)}, u32[]{:S(2)}) collective-permute-start(f32[64,512]{1,0:T(8,128)S(1)} %get-tuple-element.1140), channel_id=1, source_target_pairs={{0,16},{16,32},{32,48},{48,64},{64,80},{80,96},{96,112},{112,128},... | collective-permute-start | bytes 393224 | tf_op jit(solution)/shard_map/while/body/eval_jaxpr/ppermute | solution.py:11
  834.9 10.2 collective-permute-start.3
  845.2 11.9 %collective-permute-start.3 = (f32[64,512]{1,0:T(8,128)S(1)}, f32[64,512]{1,0:T(8,128)S(1)}, u32[]{:S(2)}, u32[]{:S(2)}) collective-permute-start(f32[64,512]{1,0:T(8,128)S(1)} %get-tuple-element.1140), channel_id=1, source_target_pairs={{0,16},{16,32},{32,48},{48,64},{64,80},{80,96},{96,112},{112,128},... | collective-permute-start | bytes 393224 | tf_op jit(solution)/shard_map/while/body/eval_jaxpr/ppermute | solution.py:11
  857.1 10.1 collective-permute-start.3
  867.2 10.7 collective-permute-start.3
  878.0 10.4 collective-permute-start.3
  888.4 11.5 %collective-permute-start.2 = (f32[64,512]{1,0:T(8,128)S(1)}, f32[64,512]{1,0:T(8,128)S(1)}, u32[]{:S(2)}, u32[]{:S(2)}) collective-permute-start(f32[64,512]{1,0:T(8,128)S(1)} %get-tuple-element.1116), channel_id=1, source_target_pairs={{0,1},{1,2},{2,3},{3,4},{4,5},{5,6},{6,7},{7,8},{8,9},{9,10},{10,1... | collective-permute-start | bytes 393224 | tf_op jit(solution)/shard_map/while/body/eval_jaxpr/ppermute | solution.py:11
  (22 other events, 511.9 us)
Sparse Core Ops, SparseCore 0:
  9.8 40.3 all-gather.6
  52.7 57.5 all-gather.4
  543.8 31.9 all-gather.10
  578.6 57.5 all-gather.8
where the time goes:
time: 1080 us
  waiting for transfers between devices  733 us (68%)
  blocking collectives  153 us (14%)
  local copies, waits for them, and re-layouts  121 us (11%)
  matrix products  28.2 us (3%)
  starting transfers between devices  21.7 us (2%)
  between operations  14.7 us (1%)
    ppermute x60, waiting for transfers between devices, passed_along(): lax.ppermute(array, axis, [(i, (i + by) % size) for i in range(size)])  546 us
    all_gather x2, waiting for transfers between devices, expand(): far_vec = lax.all_gather(vectors, 'row', axis=1, tiled=True)  114 us
    dynamic_slice x64, local copies, waits for them, and re-layouts, select_piece(): return lax.dynamic_index_in_dim(pieces, position, 1, keepdims=False)  85.8 us
    psum x1, blocking collectives, on_device(): lax.psum(jnp.stack([cross_term, resid_term, square_term]), ('row', 'col'))  76.6 us
    psum x1, blocking collectives, on_device(): rayleigh = lax.psum(first_term, ('row', 'col')) / total_rows  76.2 us
    all_gather x2, waiting for transfers between devices, expand(): near_vec = lax.all_gather(vectors, 'col', axis=1, tiled=True)  71.1 us
  transfers between devices with their start and end apart: 64, of which 64 were waited for; matrix products, arithmetic and copies ran while one was open for 8% of the time, Pallas kernels for 0%

commit v1 on v0

--- a/solution.py
+++ b/solution.py
@@ -1,9 +1,25 @@
+import functools
 import jax
 import jax.numpy as jnp
 from jax import lax
 from jax.sharding import PartitionSpec as P
 
 highest = lax.Precision.HIGHEST
+
+
+def link_widths(mine_x, join_dim):
+    return jnp.concatenate(
+        lax.all_to_all(
+            jnp.stack([mine_x for _ in range(lax.axis_size("row"))], 0),
+            axis_name="row",
+            split_axis=0,
+            concat_axis=0,
+        ),
+        join_dim,
+    )
+
+
+derive_table = functools.partial(link_widths, join_dim=1)
 
 
 def passed_along(array, axis, by):
@@ -33,7 +49,7 @@
 
     def expand(vectors):
         near_vec = lax.all_gather(vectors, "col", axis=1, tiled=True)
-        far_vec = lax.all_gather(vectors, "row", axis=1, tiled=True)
+        far_vec = derive_table(vectors)
         near_tiles = near_vec.reshape(vec_count, row_slots, tile_size)
         far_tiles = far_vec.reshape(vec_count, col_slots, tile_size)
         groups = (live_count + 7) // 8

time: 1080 us -> 1040 us (0.963)
  waiting for transfers between devices: 733 us -> 644 us
  starting transfers between devices: 21.7 us -> 62.1 us
  local copies, waits for them, and re-layouts: 121 us -> 132 us
    all_to_all x0 -> x2, waiting for transfers between devices: none -> 118 us  [link_widths(): lax.all_to_all(jnp.stack([mine_x for _ in range(lax.axis_size('row'))], 0...]
    all_gather x2 -> x0, waiting for transfers between devices: 114 us -> none  [expand(): far_vec = lax.all_gather(vectors, 'row', axis=1, tiled=True)]
    all_gather x2, waiting for transfers between devices: 71.1 us -> 0.01 us  [expand(): near_vec = lax.all_gather(vectors, 'col', axis=1, tiled=True)]
    ppermute x60, starting transfers between devices: 21.6 us -> 45.8 us  [passed_along(): lax.ppermute(array, axis, [(i, (i + by) % size) for i in range(size)])]
    ppermute x60, waiting for transfers between devices: 546 us -> 525 us  [passed_along(): lax.ppermute(array, axis, [(i, (i + by) % size) for i in range(size)])]
    all_to_all x0 -> x2, starting transfers between devices: none -> 16.2 us  [link_widths(): lax.all_to_all(jnp.stack([mine_x for _ in range(lax.axis_size('row'))], 0...]
  transfers between devices with their start and end apart: 64 -> 64, of which waited for: 64 -> 62; matrix products, arithmetic and copies ran while one was open for 8% -> 9% of each run, Pallas kernels for 0% -> 0%
where the time goes in v1:
time: 1040 us
  waiting for transfers between devices  644 us (62%)
  blocking collectives  153 us (15%)
  local copies, waits for them, and re-layouts  132 us (13%)
  starting transfers between devices  62.1 us (6%)
  matrix products  27.6 us (3%)
  between operations  15 us (1%)
    ppermute x60, waiting for transfers between devices, passed_along(): lax.ppermute(array, axis, [(i, (i + by) % size) for i in range(size)])  525 us
    all_to_all x2, waiting for transfers between devices, link_widths(): lax.all_to_all(jnp.stack([mine_x for _ in range(lax.axis_size('row'))], 0...  118 us
    dynamic_slice x64, local copies, waits for them, and re-layouts, select_piece(): return lax.dynamic_index_in_dim(pieces, position, 1, keepdims=False)  85.8 us
    psum x1, blocking collectives, on_device(): lax.psum(jnp.stack([cross_term, resid_term, square_term]), ('row', 'col'))  76.6 us
    psum x1, blocking collectives, on_device(): rayleigh = lax.psum(first_term, ('row', 'col')) / total_rows  76.2 us
    ppermute x60, starting transfers between devices, passed_along(): lax.ppermute(array, axis, [(i, (i + by) % size) for i in range(size)])  45.8 us
  transfers between devices with their start and end apart: 64, of which 62 were waited for; matrix products, arithmetic and copies ran while one was open for 9% of the time, Pallas kernels for 0%

profile of v1, /device:TPU:1, one launch (start us, length us, event | category | flops | bytes accessed | tf_op | source)
XLA Modules:
  0.0 1039.5 jit_solution(14946685328093138639)
XLA Ops:
  9.7 11.6 %all-to-all-start = ((f32[16,64,512]{2,1,0:T(8,128)}), f32[16,64,512]{2,1,0:T(8,128)S(1)}, u32[]{:S(2)}, u32[]{:S(2)}) async-start(f32[16,64,512]{2,1,0:T(8,128)} %stack.12), calls=%async_computation | async-start | bytes 4194304 | tf_op jit(solution)/shard_map/all_to_all | solution.py:12
  22.7 58.7 %all-to-all-done = f32[16,64,512]{2,1,0:T(8,128)S(1)} async-done(((f32[16,64,512]{2,1,0:T(8,128)}), f32[16,64,512]{2,1,0:T(8,128)S(1)}, u32[]{:S(2)}, u32[]{:S(2)}) %all-to-all-start) | async-done | bytes 2097184 | tf_op jit(solution)/shard_map/all_to_all | solution.py:12
  93.3 17.9 %while.84 = (s32[]{:T(128)}, f32[64,32,256]{2,1,0:T(8,128)S(1)}, f32[64,32,256]{2,1,0:T(8,128)}, s32[]{:T(128)}, s32[40]{0:T(128)S(1)}, /*index=5*/s32[40]{0:T(1...) while((s32[]{:T(128)}, f32[64,32,256]{2,1,0:T(8,128)S(1)}, ...), condition=%wide.region_1.3_spmd, body=%wide.region_0.2_spmd.sunk | while | flops 907545280 | bytes 17834760 | solution.py:90
  118.4 221.1 %while.86 = (s32[]{:T(128)}, f32[64,512]{1,0:T(8,128)S(1)}, s32[]{:T(128)}, f32[64,16,512]{2,1,0:T(8,128)}, s32[]{:T(128)}, /*index=5*/s32[]{:T(128)}, s32[]{:T(128)}, s32[]{:T(128)}) while((s32[]{:T(128)}, f32[64,512]{1,0:T(8,128)S(1)}, s32[]{:T(128)}, f32[64,16,512]{2,1,0:T(8,128)}, s32[]{:T(128)}, /*index=5*/s32[]{:T(128)}, s32[]{:T(128)}, ...), condition=%wide.region_5.7_spmd, body=%wide.region_4.6_spmd.sunk | while | flops 32785 | bytes 1179932 | solution.py:122
  120.5 77.9 %collective-permute-done.1 = f32[64,512]{1,0:T(8,128)S(1)} collective-permute-done((f32[64,512]{1,0:T(8,128)S(1)}, f32[64,512]{1,0:T(8,128)S(1)}, u32[]{:S(2)}, u32[]{:S(2)}) %collective-permute-start.1) | collective-permute-done | bytes 131104 | tf_op jit(solution)/shard_map/while/body/eval_jaxpr/ppermute | solution.py:27
  199.9 7.2 collective-permute-done.1
  208.7 8.2 collective-permute-done.1
  218.4 7.5 collective-permute-done.1
  227.4 9.6 collective-permute-done.1
  238.4 9.5 collective-permute-done.1
  249.4 10.3 collective-permute-done.1
  261.2 6.9 collective-permute-done.1
  269.6 6.7 collective-permute-done.1
  277.7 6.8 collective-permute-done.1
  286.0 7.6 collective-permute-done.1
  295.1 9.6 collective-permute-done.1
  306.2 9.1 collective-permute-done.1
  316.8 10.4 collective-permute-done.1
  328.7 10.8 %collective-permute-done.1 = f32[64,512]{1,0:T(8,128)S(1)} collective-permute-done((f32[64,512]{1,0:T(8,128)S(1)}, f32[64,512]{1,0:T(8,128)S(1)}, u32[]{:S(2)}, u32[]{:S(2)}) %collective-permute-start.1) | collective-permute-done | bytes 131104 | tf_op jit(solution)/shard_map/while/body/eval_jaxpr/ppermute | solution.py:27
  339.6 105.6 %while.85 = (s32[]{:T(128)}, f32[64,512]{1,0:T(8,128)S(1)}, s32[]{:T(128)}, f32[64,16,512]{2,1,0:T(8,128)}, s32[]{:T(128)}, /*index=5*/s32[]{:T(128)}, s32[]{:T(128)}, s32[]{:T(128)}) while((s32[]{:T(128)}, f32[64,512]{1,0:T(8,128)S(1)}, s32[]{:T(128)}, f32[64,16,512]{2,1,0:T(8,128)}, s32[]{:T(128)}, /*index=5*/s32[]{:T(128)}, s32[]{:T(128)}, ...), condition=%wide.region_3.5_spmd, body=%wide.region_2.4_spmd.sunk | while | flops 32785 | bytes 1179932 | solution.py:121
  339.6 13.1 %collective-permute-start = (f32[64,512]{1,0:T(8,128)S(1)}, f32[64,512]{1,0:T(8,128)S(1)}, u32[]{:S(2)}, u32[]{:S(2)}) collective-permute-start(f32[64,512]{1,0:T(8,128)S(1)} %get-tuple-element.1065), channel_id=1, source_target_pairs={{0,1},{1,2},{2,3},{3,4},{4,5},{5,6},{6,7},{7,8},{8,9},{9,10},{10,1... | collective-permute-start | bytes 393224 | tf_op jit(solution)/shard_map/while/body/eval_jaxpr/ppermute | solution.py:27
  373.9 5.1 collective-permute-done
  380.5 5.1 collective-permute-done
  387.1 5.1 collective-permute-done
  393.7 5.1 collective-permute-done
  400.3 5.1 collective-permute-done
  445.5 76.2 %psum.14 = f32[64,64]{0,1:T(8,128)S(1)} all-reduce(f32[64,64]{0,1:T(8,128)S(1)} %convolution_bitcast_fusion.3), channel_id=1, replica_groups=mesh['row'=16,'col'=16] {'row','col'}, use_global_device_ids=true, to_apply=%region_6.8 | all-reduce | flops 4096 | bytes 32768 | tf_op jit(solution)/shard_map/psum | solution.py:128
  530.3 58.8 %all-to-all-done.1 = f32[16,64,512]{2,1,0:T(8,128)S(1)} async-done(((f32[16,64,512]{2,1,0:T(8,128)}), f32[16,64,512]{2,1,0:T(8,128)S(1)}, u32[]{:S(2)}, u32[]{:S(2)}) %all-to-all-start.1) | async-done | bytes 2097184 | tf_op jit(solution)/shard_map/all_to_all | solution.py:12
  600.9 17.8 %while.87 = (s32[]{:T(128)}, f32[64,32,256]{2,1,0:T(8,128)S(1)}, f32[64,32,256]{2,1,0:T(8,128)}, s32[]{:T(128)}, s32[40]{0:T(128)S(1)}, /*index=5*/s32[40]{0:T(1...) while((s32[]{:T(128)}, f32[64,32,256]{2,1,0:T(8,128)S(1)}, ...), condition=%wide.region_8.10_spmd, body=%wide.region_7.9_spmd.sunk | while | flops 907545280 | bytes 17834760 | solution.py:90
  625.9 225.1 %while.89 = (s32[]{:T(128)}, f32[64,512]{1,0:T(8,128)S(1)}, s32[]{:T(128)}, f32[64,16,512]{2,1,0:T(8,128)}, s32[]{:T(128)}, /*index=5*/s32[]{:T(128)}, s32[]{:T(128)}, s32[]{:T(128)}) while((s32[]{:T(128)}, f32[64,512]{1,0:T(8,128)S(1)}, s32[]{:T(128)}, f32[64,16,512]{2,1,0:T(8,128)}, s32[]{:T(128)}, /*index=5*/s32[]{:T(128)}, s32[]{:T(128)}, ...), condition=%wide.region_12.14_spmd, body=%wide.region_11.13_spmd.sunk | while | flops 32785 | bytes 1179932 | solution.py:122
  627.3 77.3 %collective-permute-done.3 = f32[64,512]{1,0:T(8,128)S(1)} collective-permute-done((f32[64,512]{1,0:T(8,128)S(1)}, f32[64,512]{1,0:T(8,128)S(1)}, u32[]{:S(2)}, u32[]{:S(2)}) %collective-permute-start.3) | collective-permute-done | bytes 131104 | tf_op jit(solution)/shard_map/while/body/eval_jaxpr/ppermute | solution.py:27
  706.2 10.5 %collective-permute-done.3 = f32[64,512]{1,0:T(8,128)S(1)} collective-permute-done((f32[64,512]{1,0:T(8,128)S(1)}, f32[64,512]{1,0:T(8,128)S(1)}, u32[]{:S(2)}, u32[]{:S(2)}) %collective-permute-start.3) | collective-permute-done | bytes 131104 | tf_op jit(solution)/shard_map/while/body/eval_jaxpr/ppermute | solution.py:27
  718.1 10.1 collective-permute-done.3
  729.7 10.0 collective-permute-done.3
  741.1 8.8 collective-permute-done.3
  751.4 9.7 collective-permute-done.3
  762.6 6.7 collective-permute-done.3
  770.7 6.7 collective-permute-done.3
  778.9 6.7 collective-permute-done.3
  787.0 8.5 collective-permute-done.3
  797.1 10.4 collective-permute-done.3
  809.0 6.7 collective-permute-done.3
  817.2 10.0 collective-permute-done.3
  828.6 9.8 collective-permute-done.3
  839.9 11.0 %collective-permute-done.3 = f32[64,512]{1,0:T(8,128)S(1)} collective-permute-done((f32[64,512]{1,0:T(8,128)S(1)}, f32[64,512]{1,0:T(8,128)S(1)}, u32[]{:S(2)}, u32[]{:S(2)}) %collective-permute-start.3) | collective-permute-done | bytes 131104 | tf_op jit(solution)/shard_map/while/body/eval_jaxpr/ppermute | solution.py:27
  850.9 103.7 %while.88 = (s32[]{:T(128)}, f32[64,512]{1,0:T(8,128)S(1)}, s32[]{:T(128)}, f32[64,16,512]{2,1,0:T(8,128)}, s32[]{:T(128)}, /*index=5*/s32[]{:T(128)}, s32[]{:T(128)}, s32[]{:T(128)}) while((s32[]{:T(128)}, f32[64,512]{1,0:T(8,128)S(1)}, s32[]{:T(128)}, f32[64,16,512]{2,1,0:T(8,128)}, s32[]{:T(128)}, /*index=5*/s32[]{:T(128)}, s32[]{:T(128)}, ...), condition=%wide.region_10.12_spmd, body=%wide.region_9.11_spmd.sunk | while | flops 32785 | bytes 1179932 | solution.py:121
  851.0 13.8 %collective-permute-start.2 = (f32[64,512]{1,0:T(8,128)S(1)}, f32[64,512]{1,0:T(8,128)S(1)}, u32[]{:S(2)}, u32[]{:S(2)}) collective-permute-start(f32[64,512]{1,0:T(8,128)S(1)} %get-tuple-element.1155), channel_id=1, source_target_pairs={{0,1},{1,2},{2,3},{3,4},{4,5},{5,6},{6,7},{7,8},{8,9},{9,10},{10,1... | collective-permute-start | bytes 393224 | tf_op jit(solution)/shard_map/while/body/eval_jaxpr/ppermute | solution.py:27
  955.3 76.6 %psum.15 = f32[3,64,64]{1,2,0:T(8,128)S(1)} all-reduce(f32[3,64,64]{1,2,0:T(8,128)S(1)} %pad_maximum_fusion.1), channel_id=1, replica_groups=mesh['row'=16,'col'=16] {'row','col'}, use_global_device_ids=true, to_apply=%region_13.15 | all-reduce | flops 12288 | bytes 98304 | tf_op jit(solution)/shard_map/psum | solution.py:137
  (286 shorter events, 286.3 us)
Async XLA Ops:
  9.7 71.7 %all-to-all-start = ((f32[16,64,512]{2,1,0:T(8,128)}), f32[16,64,512]{2,1,0:T(8,128)S(1)}, u32[]{:S(2)}, u32[]{:S(2)}) async-start(f32[16,64,512]{2,1,0:T(8,128)} %stack.12), calls=%async_computation | async-start | bytes 4194304 | tf_op jit(solution)/shard_map/all_to_all | solution.py:12
  21.2 67.0 %all-gather.3.cloned.1.call-start = ((), (), s32[]{:S(2)}) async-start(), calls=%async_computation.2 | async-start | bytes 2228224 | tf_op jit(solution)/shard_map/all_gather | solution.py:51
  118.4 80.0 %collective-permute-start.1 = (f32[64,512]{1,0:T(8,128)S(1)}, f32[64,512]{1,0:T(8,128)S(1)}, u32[]{:S(2)}, u32[]{:S(2)}) collective-permute-start(f32[64,512]{1,0:T(8,128)S(1)} %get-tuple-element.1089), channel_id=1, source_target_pairs={{0,16},{16,32},{32,48},{48,64},{64,80},{80,96},{96,112},{112,128},... | collective-permute-start | bytes 393224 | tf_op jit(solution)/shard_map/while/body/eval_jaxpr/ppermute | solution.py:27
  198.5 8.7 collective-permute-start.1
  207.2 9.7 collective-permute-start.1
  216.9 9.0 collective-permute-start.1
  225.9 11.0 %collective-permute-start.1 = (f32[64,512]{1,0:T(8,128)S(1)}, f32[64,512]{1,0:T(8,128)S(1)}, u32[]{:S(2)}, u32[]{:S(2)}) collective-permute-start(f32[64,512]{1,0:T(8,128)S(1)} %get-tuple-element.1089), channel_id=1, source_target_pairs={{0,16},{16,32},{32,48},{48,64},{64,80},{80,96},{96,112},{112,128},... | collective-permute-start | bytes 393224 | tf_op jit(solution)/shard_map/while/body/eval_jaxpr/ppermute | solution.py:27
  237.0 10.9 %collective-permute-start.1 = (f32[64,512]{1,0:T(8,128)S(1)}, f32[64,512]{1,0:T(8,128)S(1)}, u32[]{:S(2)}, u32[]{:S(2)}) collective-permute-start(f32[64,512]{1,0:T(8,128)S(1)} %get-tuple-element.1089), channel_id=1, source_target_pairs={{0,16},{16,32},{32,48},{48,64},{64,80},{80,96},{96,112},{112,128},... | collective-permute-start | bytes 393224 | tf_op jit(solution)/shard_map/while/body/eval_jaxpr/ppermute | solution.py:27
  247.9 11.8 %collective-permute-start.1 = (f32[64,512]{1,0:T(8,128)S(1)}, f32[64,512]{1,0:T(8,128)S(1)}, u32[]{:S(2)}, u32[]{:S(2)}) collective-permute-start(f32[64,512]{1,0:T(8,128)S(1)} %get-tuple-element.1089), channel_id=1, source_target_pairs={{0,16},{16,32},{32,48},{48,64},{64,80},{80,96},{96,112},{112,128},... | collective-permute-start | bytes 393224 | tf_op jit(solution)/shard_map/while/body/eval_jaxpr/ppermute | solution.py:27
  259.8 8.3 collective-permute-start.1
  268.1 8.1 collective-permute-start.1
  276.3 8.2 collective-permute-start.1
  284.5 9.1 collective-permute-start.1
  293.6 11.1 %collective-permute-start.1 = (f32[64,512]{1,0:T(8,128)S(1)}, f32[64,512]{1,0:T(8,128)S(1)}, u32[]{:S(2)}, u32[]{:S(2)}) collective-permute-start(f32[64,512]{1,0:T(8,128)S(1)} %get-tuple-element.1089), channel_id=1, source_target_pairs={{0,16},{16,32},{32,48},{48,64},{64,80},{80,96},{96,112},{112,128},... | collective-permute-start | bytes 393224 | tf_op jit(solution)/shard_map/while/body/eval_jaxpr/ppermute | solution.py:27
  304.7 10.6 %collective-permute-start.1 = (f32[64,512]{1,0:T(8,128)S(1)}, f32[64,512]{1,0:T(8,128)S(1)}, u32[]{:S(2)}, u32[]{:S(2)}) collective-permute-start(f32[64,512]{1,0:T(8,128)S(1)} %get-tuple-element.1089), channel_id=1, source_target_pairs={{0,16},{16,32},{32,48},{48,64},{64,80},{80,96},{96,112},{112,128},... | collective-permute-start | bytes 393224 | tf_op jit(solution)/shard_map/while/body/eval_jaxpr/ppermute | solution.py:27
  315.4 11.8 %collective-permute-start.1 = (f32[64,512]{1,0:T(8,128)S(1)}, f32[64,512]{1,0:T(8,128)S(1)}, u32[]{:S(2)}, u32[]{:S(2)}) collective-permute-start(f32[64,512]{1,0:T(8,128)S(1)} %get-tuple-element.1089), channel_id=1, source_target_pairs={{0,16},{16,32},{32,48},{48,64},{64,80},{80,96},{96,112},{112,128},... | collective-permute-start | bytes 393224 | tf_op jit(solution)/shard_map/while/body/eval_jaxpr/ppermute | solution.py:27
  327.2 12.3 %collective-permute-start.1 = (f32[64,512]{1,0:T(8,128)S(1)}, f32[64,512]{1,0:T(8,128)S(1)}, u32[]{:S(2)}, u32[]{:S(2)}) collective-permute-start(f32[64,512]{1,0:T(8,128)S(1)} %get-tuple-element.1089), channel_id=1, source_target_pairs={{0,16},{16,32},{32,48},{48,64},{64,80},{80,96},{96,112},{112,128},... | collective-permute-start | bytes 393224 | tf_op jit(solution)/shard_map/while/body/eval_jaxpr/ppermute | solution.py:27
  339.6 15.1 %collective-permute-start = (f32[64,512]{1,0:T(8,128)S(1)}, f32[64,512]{1,0:T(8,128)S(1)}, u32[]{:S(2)}, u32[]{:S(2)}) collective-permute-start(f32[64,512]{1,0:T(8,128)S(1)} %get-tuple-element.1065), channel_id=1, source_target_pairs={{0,1},{1,2},{2,3},{3,4},{4,5},{5,6},{6,7},{7,8},{8,9},{9,10},{10,1... | collective-permute-start | bytes 393224 | tf_op jit(solution)/shard_map/while/body/eval_jaxpr/ppermute | solution.py:27
  365.8 6.6 collective-permute-start
  372.4 6.6 collective-permute-start
  379.0 6.6 collective-permute-start
  385.6 6.6 collective-permute-start
  392.2 6.6 collective-permute-start
  398.9 6.6 collective-permute-start
  405.5 6.6 collective-permute-start
  412.1 6.6 collective-permute-start
  418.7 6.6 collective-permute-start
  425.3 6.6 collective-permute-start
  431.9 6.6 collective-permute-start
  438.5 6.6 collective-permute-start
  523.6 65.4 %all-to-all-start.1 = ((f32[16,64,512]{2,1,0:T(8,128)}), f32[16,64,512]{2,1,0:T(8,128)S(1)}, u32[]{:S(2)}, u32[]{:S(2)}) async-start(f32[16,64,512]{2,1,0:T(8,128)} %stack.13), calls=%async_computation.1 | async-start | bytes 4194304 | tf_op jit(solution)/shard_map/all_to_all | solution.py:12
  528.2 67.6 %all-gather.5.cloned.1.call-start = ((), (), s32[]{:S(2)}) async-start(), calls=%async_computation.3 | async-start | bytes 2228224 | tf_op jit(solution)/shard_map/all_gather | solution.py:51
  625.9 78.8 %collective-permute-start.3 = (f32[64,512]{1,0:T(8,128)S(1)}, f32[64,512]{1,0:T(8,128)S(1)}, u32[]{:S(2)}, u32[]{:S(2)}) collective-permute-start(f32[64,512]{1,0:T(8,128)S(1)} %get-tuple-element.1179), channel_id=1, source_target_pairs={{0,16},{16,32},{32,48},{48,64},{64,80},{80,96},{96,112},{112,128},... | collective-permute-start | bytes 393224 | tf_op jit(solution)/shard_map/while/body/eval_jaxpr/ppermute | solution.py:27
  704.7 11.9 %collective-permute-start.3 = (f32[64,512]{1,0:T(8,128)S(1)}, f32[64,512]{1,0:T(8,128)S(1)}, u32[]{:S(2)}, u32[]{:S(2)}) collective-permute-start(f32[64,512]{1,0:T(8,128)S(1)} %get-tuple-element.1179), channel_id=1, source_target_pairs={{0,16},{16,32},{32,48},{48,64},{64,80},{80,96},{96,112},{112,128},... | collective-permute-start | bytes 393224 | tf_op jit(solution)/shard_map/while/body/eval_jaxpr/ppermute | solution.py:27
  716.7 11.5 %collective-permute-start.3 = (f32[64,512]{1,0:T(8,128)S(1)}, f32[64,512]{1,0:T(8,128)S(1)}, u32[]{:S(2)}, u32[]{:S(2)}) collective-permute-start(f32[64,512]{1,0:T(8,128)S(1)} %get-tuple-element.1179), channel_id=1, source_target_pairs={{0,16},{16,32},{32,48},{48,64},{64,80},{80,96},{96,112},{112,128},... | collective-permute-start | bytes 393224 | tf_op jit(solution)/shard_map/while/body/eval_jaxpr/ppermute | solution.py:27
  728.2 11.4 %collective-permute-start.3 = (f32[64,512]{1,0:T(8,128)S(1)}, f32[64,512]{1,0:T(8,128)S(1)}, u32[]{:S(2)}, u32[]{:S(2)}) collective-permute-start(f32[64,512]{1,0:T(8,128)S(1)} %get-tuple-element.1179), channel_id=1, source_target_pairs={{0,16},{16,32},{32,48},{48,64},{64,80},{80,96},{96,112},{112,128},... | collective-permute-start | bytes 393224 | tf_op jit(solution)/shard_map/while/body/eval_jaxpr/ppermute | solution.py:27
  739.7 10.2 collective-permute-start.3
  749.9 11.1 %collective-permute-start.3 = (f32[64,512]{1,0:T(8,128)S(1)}, f32[64,512]{1,0:T(8,128)S(1)}, u32[]{:S(2)}, u32[]{:S(2)}) collective-permute-start(f32[64,512]{1,0:T(8,128)S(1)} %get-tuple-element.1179), channel_id=1, source_target_pairs={{0,16},{16,32},{32,48},{48,64},{64,80},{80,96},{96,112},{112,128},... | collective-permute-start | bytes 393224 | tf_op jit(solution)/shard_map/while/body/eval_jaxpr/ppermute | solution.py:27
  761.1 8.2 collective-permute-start.3
  769.3 8.1 collective-permute-start.3
  777.4 8.1 collective-permute-start.3
  785.6 10.0 collective-permute-start.3
  795.6 11.9 %collective-permute-start.3 = (f32[64,512]{1,0:T(8,128)S(1)}, f32[64,512]{1,0:T(8,128)S(1)}, u32[]{:S(2)}, u32[]{:S(2)}) collective-permute-start(f32[64,512]{1,0:T(8,128)S(1)} %get-tuple-element.1179), channel_id=1, source_target_pairs={{0,16},{16,32},{32,48},{48,64},{64,80},{80,96},{96,112},{112,128},... | collective-permute-start | bytes 393224 | tf_op jit(solution)/shard_map/while/body/eval_jaxpr/ppermute | solution.py:27
  807.5 8.2 collective-permute-start.3
  815.7 11.4 %collective-permute-start.3 = (f32[64,512]{1,0:T(8,128)S(1)}, f32[64,512]{1,0:T(8,128)S(1)}, u32[]{:S(2)}, u32[]{:S(2)}) collective-permute-start(f32[64,512]{1,0:T(8,128)S(1)} %get-tuple-element.1179), channel_id=1, source_target_pairs={{0,16},{16,32},{32,48},{48,64},{64,80},{80,96},{96,112},{112,128},... | collective-permute-start | bytes 393224 | tf_op jit(solution)/shard_map/while/body/eval_jaxpr/ppermute | solution.py:27
  827.2 11.2 %collective-permute-start.3 = (f32[64,512]{1,0:T(8,128)S(1)}, f32[64,512]{1,0:T(8,128)S(1)}, u32[]{:S(2)}, u32[]{:S(2)}) collective-permute-start(f32[64,512]{1,0:T(8,128)S(1)} %get-tuple-element.1179), channel_id=1, source_target_pairs={{0,16},{16,32},{32,48},{48,64},{64,80},{80,96},{96,112},{112,128},... | collective-permute-start | bytes 393224 | tf_op jit(solution)/shard_map/while/body/eval_jaxpr/ppermute | solution.py:27
  838.4 12.5 %collective-permute-start.3 = (f32[64,512]{1,0:T(8,128)S(1)}, f32[64,512]{1,0:T(8,128)S(1)}, u32[]{:S(2)}, u32[]{:S(2)}) collective-permute-start(f32[64,512]{1,0:T(8,128)S(1)} %get-tuple-element.1179), channel_id=1, source_target_pairs={{0,16},{16,32},{32,48},{48,64},{64,80},{80,96},{96,112},{112,128},... | collective-permute-start | bytes 393224 | tf_op jit(solution)/shard_map/while/body/eval_jaxpr/ppermute | solution.py:27
  851.0 15.8 %collective-permute-start.2 = (f32[64,512]{1,0:T(8,128)S(1)}, f32[64,512]{1,0:T(8,128)S(1)}, u32[]{:S(2)}, u32[]{:S(2)}) collective-permute-start(f32[64,512]{1,0:T(8,128)S(1)} %get-tuple-element.1155), channel_id=1, source_target_pairs={{0,1},{1,2},{2,3},{3,4},{4,5},{5,6},{6,7},{7,8},{8,9},{9,10},{10,1... | collective-permute-start | bytes 393224 | tf_op jit(solution)/shard_map/while/body/eval_jaxpr/ppermute | solution.py:27
  (23 other events, 469.6 us)
Sparse Core Ops, SparseCore 0:
  23.8 52.5 all-gather.2
  531.4 51.1 all-gather.4
